TPU v7x, 512 devices: a whole 4x8x8 slice. The times are simulated.
512 devices in a mesh: blade: 4 (over z_hi), grid: 128 (over y, z_lo, x, core).
Axes of the slice: x: 4, y: 8, z: 8 (z_hi: 4, z_lo: 2; z = z_hi * 2 + z_lo), core: 2. Of those that a mesh axis runs over, the one named last changes fastest.
Arguments:
- modal_blocks: float32 [4, 3072, 3, 16, 128], P('blade', 'grid'), may hold values from -4 to 4
- amplitudes: float32 [4, 24], P('blade'), may hold values from 0.2 to 1
- owner_map: int32 [4], P('blade'), may hold values from 0 to 127
- span_interp: float32 [4, 16, 4096], P('blade', None, 'grid'), may hold values from -1.5 to 1.5
- chord_interp: float32 [4, 16384, 256], P('blade', 'grid'), may hold values from -0.5 to 0.5
- base_coords: float32 [4, 3, 4096, 256], P('blade', None, 'grid'), may hold values from -6 to 6
- flow_state: float32 [4, 3, 4096, 256], P('blade', None, 'grid'), may hold values from -6 to 6
- face_rows: int32 [4, 12288], P('blade', 'grid'), may hold values from 0 to 31
- face_owner: int32 [4, 12288, 1], P('blade', 'grid'), may hold values from 0 to 127; in each aligned block of 96 rows (0 to 95, 96 to 191, ..., all dimensions but the last counted through in order) at most 2 rows name the same one
Outputs:
- residual: float32 [4, 4096, 256], P('blade', 'grid')
- fringe_faces: float32 [4, 32768, 3, 256], P('blade', 'grid')
Inputs may be any that keep to these rules, and one draw needn't show every extreme that they name: `face_owner`: in the 96 faces of one grid block, no receiver is named more than 2 times, and some block names one receiver exactly 2 times.
All inputs are finite; a program needn't handle non-finite values.
Results may differ from a plain program's by a relative error of at most 0.0003.
Values sent between devices are 32-bit elements; how exact they have to be, the bound alone decides.
A program may use at most 64 MiB of HBM per device.

v0:
```python
import jax
import jax.numpy as jnp
from jax import lax
from jax.sharding import PartitionSpec as P

CAP = 2


ALPHA_SIDE = 1.0 / 3.0
FIRST_COEF = 7.0 / 9.0
SECOND_COEF = 1.0 / 36.0


def spread(value, axis, source):
    kept = jnp.where(lax.axis_index(axis) == source, value, 0).astype(value.dtype)
    return lax.psum(kept, axis)


def compact_operator(count):
    positions = jnp.arange(count)
    offset = positions[None, :] - positions[:, None]
    bmatrix = (
        jnp.where(offset == 1, FIRST_COEF, 0.0)
        - jnp.where(offset == -1, FIRST_COEF, 0.0)
        + jnp.where(offset == 2, SECOND_COEF, 0.0)
        - jnp.where(offset == -2, SECOND_COEF, 0.0)
    ).astype(jnp.float32)
    below_diag = jnp.where(positions > 0, ALPHA_SIDE, 0.0).astype(jnp.float32)
    above_diag = jnp.where(positions < count - 1, ALPHA_SIDE, 0.0).astype(jnp.float32)
    middle = jnp.ones((count,), jnp.float32)
    return lax.linalg.tridiagonal_solve(below_diag, middle, above_diag, bmatrix)


def derive_rows(matrix, field):
    return jnp.einsum("ik,...kj->...ij", matrix, field, precision=lax.Precision.HIGHEST)


def derive_cols(matrix, field):
    return jnp.einsum("jk,...ik->...ij", matrix, field, precision=lax.Precision.HIGHEST)


def cross_three(first, second):
    return jnp.stack(
        [
            first[1] * second[2] - first[2] * second[1],
            first[2] * second[0] - first[0] * second[2],
            first[0] * second[1] - first[1] * second[0],
        ]
    )


def flux_divergence(coords, flow, op_rows, op_cols):
    along_rows = derive_rows(op_rows, coords)
    along_cols = derive_cols(op_cols, coords)
    normal = cross_three(along_rows, along_cols)
    weight = 1.0 + jnp.sum(normal * normal, axis=0)
    flux_rows = jnp.sum(flow * cross_three(along_cols, normal), axis=0) / weight
    flux_cols = jnp.sum(flow * cross_three(normal, along_rows), axis=0) / weight
    return derive_rows(op_rows, flux_rows) + derive_cols(op_cols, flux_cols)


def body(
    modal_blocks,
    amplitudes,
    owner_map,
    span_interp,
    chord_interp,
    base_coords,
    flow_state,
    face_rows,
    face_owner,
):
    scaled = amplitudes[0][:, None, None, None] * modal_blocks[0]
    root = owner_map[0]
    received = spread(scaled, "grid", root)
    shape_sum = jnp.sum(received, axis=0)
    spanwise = jnp.einsum("sr,cst->crt", span_interp[0], shape_sum, precision=lax.Precision.HIGHEST)
    displace = jnp.einsum("crt,tj->crj", spanwise, chord_interp[0], precision=lax.Precision.HIGHEST)
    coords = base_coords[0] + displace
    rows_local = coords.shape[1]
    width = coords.shape[2]
    peers = lax.axis_size("grid")
    count_faces = face_rows.shape[1]
    picker = (face_rows[0][:, None] == jnp.arange(rows_local, dtype=jnp.int32)[None, :]).astype(
        jnp.float32
    )
    faces = jnp.einsum("fi,cij->fcj", picker, coords, precision=lax.Precision.HIGHEST)
    target = face_owner[0, :, 0]
    order = jnp.arange(count_faces)
    earlier = (target[:, None] == target[None, :]) & (order[None, :] < order[:, None])
    slot = jnp.sum(earlier.astype(jnp.int32), axis=1)
    place = target * CAP + slot
    table = (place[None, :] == jnp.arange(peers * CAP, dtype=jnp.int32)[:, None]).astype(
        jnp.float32
    )
    outgoing = jnp.einsum("pf,fcj->pcj", table, faces, precision=lax.Precision.HIGHEST)
    outgoing = outgoing.reshape(peers, CAP, 3, width)
    arrived = lax.all_to_all(outgoing, "grid", split_axis=0, concat_axis=0, tiled=True)
    fringe = arrived.reshape(1, peers * CAP, 3, width)
    op_rows = compact_operator(rows_local)
    op_cols = compact_operator(width)
    result = flux_divergence(coords, flow_state[0], op_rows, op_cols)
    return (result[None], fringe)


def solution(mesh):
    return jax.shard_map(
        body,
        mesh=mesh,
        in_specs=(
            P("blade", "grid", None, None, None),
            P("blade", None),
            P("blade"),
            P("blade", None, "grid"),
            P("blade", "grid", None),
            P("blade", None, "grid", None),
            P("blade", None, "grid", None),
            P("blade", "grid"),
            P("blade", "grid", None),
        ),
        out_specs=(P("blade", "grid", None), P("blade", "grid", None, None)),
        check_vma=False,
    )
```

profile of v0, /device:TPU:1, one launch (start us, length us, event | category | flops | bytes accessed | tf_op | source)
XLA Modules:
  0.0 1079.0 jit_solution(11147028896832815861)
XLA Ops:
  8.6 2.0 fusion.1
  16.8 449.2 %while.32 = (s32[]{:T(128)}, f32[]{:T(128)}, f32[256]{0:T(256)S(1)}, f32[7,32]{1,0:T(8,128)S(1)}, f32[7,32,256]{2,1,0:T(8,128)S(1)}, /*index=5*/f32[7,32]{1,0:T(...) while((s32[]{:T(128)}, f32[]{:T(128)}, ...), condition=%wide.region_3.4_spmd, body=%wide.region_2.3_spmd.sunk | while | flops 24705 | bytes 269049 | solution.py:31
  60.5 19.8 %subtract_divide_fusion.125 = (f32[256]{0:T(256)S(1)}, f32[256]{0:T(256)S(1)}, f32[256]{0:T(256)S(1)}, f32[256]{0:T(256)S(1)}, f32[256]{0:T(256)S(1)}, /*index=5...) fusion(f32[256]{0:T(256)S(1)} %bitcast.1203, ...), kind=kLoop, calls=%fused_computation.35.clone.1 | loop fusion | flops 24576 | bytes 66816 | tf_op jit(solution)/shard_map/while/body/eval_jaxpr/div | solution.py:31
  124.7 19.8 %subtract_divide_fusion.125 = (f32[256]{0:T(256)S(1)}, f32[256]{0:T(256)S(1)}, f32[256]{0:T(256)S(1)}, f32[256]{0:T(256)S(1)}, f32[256]{0:T(256)S(1)}, /*index=5...) fusion(f32[256]{0:T(256)S(1)} %bitcast.1203, ...), kind=kLoop, calls=%fused_computation.35.clone.1 | loop fusion | flops 24576 | bytes 66816 | tf_op jit(solution)/shard_map/while/body/eval_jaxpr/div | solution.py:31
  188.8 19.8 %subtract_divide_fusion.125 = (f32[256]{0:T(256)S(1)}, f32[256]{0:T(256)S(1)}, f32[256]{0:T(256)S(1)}, f32[256]{0:T(256)S(1)}, f32[256]{0:T(256)S(1)}, /*index=5...) fusion(f32[256]{0:T(256)S(1)} %bitcast.1203, ...), kind=kLoop, calls=%fused_computation.35.clone.1 | loop fusion | flops 24576 | bytes 66816 | tf_op jit(solution)/shard_map/while/body/eval_jaxpr/div | solution.py:31
  253.0 19.8 %subtract_divide_fusion.125 = (f32[256]{0:T(256)S(1)}, f32[256]{0:T(256)S(1)}, f32[256]{0:T(256)S(1)}, f32[256]{0:T(256)S(1)}, f32[256]{0:T(256)S(1)}, /*index=5...) fusion(f32[256]{0:T(256)S(1)} %bitcast.1203, ...), kind=kLoop, calls=%fused_computation.35.clone.1 | loop fusion | flops 24576 | bytes 66816 | tf_op jit(solution)/shard_map/while/body/eval_jaxpr/div | solution.py:31
  317.2 19.8 %subtract_divide_fusion.125 = (f32[256]{0:T(256)S(1)}, f32[256]{0:T(256)S(1)}, f32[256]{0:T(256)S(1)}, f32[256]{0:T(256)S(1)}, f32[256]{0:T(256)S(1)}, /*index=5...) fusion(f32[256]{0:T(256)S(1)} %bitcast.1203, ...), kind=kLoop, calls=%fused_computation.35.clone.1 | loop fusion | flops 24576 | bytes 66816 | tf_op jit(solution)/shard_map/while/body/eval_jaxpr/div | solution.py:31
  381.3 19.8 %subtract_divide_fusion.125 = (f32[256]{0:T(256)S(1)}, f32[256]{0:T(256)S(1)}, f32[256]{0:T(256)S(1)}, f32[256]{0:T(256)S(1)}, f32[256]{0:T(256)S(1)}, /*index=5...) fusion(f32[256]{0:T(256)S(1)} %bitcast.1203, ...), kind=kLoop, calls=%fused_computation.35.clone.1 | loop fusion | flops 24576 | bytes 66816 | tf_op jit(solution)/shard_map/while/body/eval_jaxpr/div | solution.py:31
  445.5 19.8 %subtract_divide_fusion.125 = (f32[256]{0:T(256)S(1)}, f32[256]{0:T(256)S(1)}, f32[256]{0:T(256)S(1)}, f32[256]{0:T(256)S(1)}, f32[256]{0:T(256)S(1)}, /*index=5...) fusion(f32[256]{0:T(256)S(1)} %bitcast.1203, ...), kind=kLoop, calls=%fused_computation.35.clone.1 | loop fusion | flops 24576 | bytes 66816 | tf_op jit(solution)/shard_map/while/body/eval_jaxpr/div | solution.py:31
  505.1 18.7 %fusion.35 = (f32[1,32]{1,0:T(1,128)S(1)}, f32[1,32]{1,0:T(1,128)S(1)}, f32[1,32]{1,0:T(1,128)S(1)}, f32[1,32]{1,0:T(1,128)S(1)}, f32[1,32]{1,0:T(1,128)S(1)}, /...) fusion(f32[32,32]{1,0:T(8,128)S(1)} %select_subtract_fusion.1, ...), kind=kLoop, calls=%fused_computation.259 | loop fusion | flops 2880 | bytes 8048 | tf_op jit(solution)/shard_map/eval_jaxpr/div | solution.py:31
  563.4 0.8 concatenate.29
  564.3 19.3 %subtract_divide_fusion.32 = (f32[256]{0:T(256)S(1)}, f32[256]{0:T(256)S(1)}, f32[256]{0:T(256)S(1)}, f32[256]{0:T(256)S(1)}, f32[256]{0:T(256)S(1)}, /*index=5*...) fusion(f32[256]{0:T(256)S(1)} %bitcast.1408, ...), kind=kLoop, calls=%fused_computation.225 | loop fusion | flops 23808 | bytes 64760 | tf_op jit(solution)/shard_map/eval_jaxpr/div | solution.py:31
  583.8 151.6 %while.33 = (s32[]{:T(128)}, f32[256]{0:T(256)S(1)}, f32[7,32,256]{2,1,0:T(8,128)S(1)}, f32[7,32,256]{2,1,0:T(8,128)S(1)}, f32[7,32]{1,0:T(8,128)S(1)}, /*index=...) while((s32[]{:T(128)}, f32[256]{0:T(256)S(1)}, ...), condition=%wide.region_5.6_spmd, body=%wide.region_4.5_spmd.sunk | while | flops 16418 | bytes 266713 | solution.py:31
  584.6 0.7 fusion.136
  585.5 19.9 %multiply_subtract_fusion.198 = (f32[256]{0:T(256)S(1)}, f32[256]{0:T(256)S(1)}, f32[256]{0:T(256)S(1)}, f32[256]{0:T(256)S(1)}, f32[256]{0:T(256)S(1)}, /*index...) fusion(f32[256]{0:T(256)S(1)} %bitcast.1284, ...), kind=kLoop, calls=%fused_computation.101.clone.1 | loop fusion | flops 16384 | bytes 66688 | tf_op jit(solution)/shard_map/while/body/eval_jaxpr/sub | solution.py:31
  606.3 0.7 fusion.136
  607.1 19.9 %multiply_subtract_fusion.198 = (f32[256]{0:T(256)S(1)}, f32[256]{0:T(256)S(1)}, f32[256]{0:T(256)S(1)}, f32[256]{0:T(256)S(1)}, f32[256]{0:T(256)S(1)}, /*index...) fusion(f32[256]{0:T(256)S(1)} %bitcast.1284, ...), kind=kLoop, calls=%fused_computation.101.clone.1 | loop fusion | flops 16384 | bytes 66688 | tf_op jit(solution)/shard_map/while/body/eval_jaxpr/sub | solution.py:31
  628.8 19.9 %multiply_subtract_fusion.198 = (f32[256]{0:T(256)S(1)}, f32[256]{0:T(256)S(1)}, f32[256]{0:T(256)S(1)}, f32[256]{0:T(256)S(1)}, f32[256]{0:T(256)S(1)}, /*index...) fusion(f32[256]{0:T(256)S(1)} %bitcast.1284, ...), kind=kLoop, calls=%fused_computation.101.clone.1 | loop fusion | flops 16384 | bytes 66688 | tf_op jit(solution)/shard_map/while/body/eval_jaxpr/sub | solution.py:31
  650.4 19.9 %multiply_subtract_fusion.198 = (f32[256]{0:T(256)S(1)}, f32[256]{0:T(256)S(1)}, f32[256]{0:T(256)S(1)}, f32[256]{0:T(256)S(1)}, f32[256]{0:T(256)S(1)}, /*index...) fusion(f32[256]{0:T(256)S(1)} %bitcast.1284, ...), kind=kLoop, calls=%fused_computation.101.clone.1 | loop fusion | flops 16384 | bytes 66688 | tf_op jit(solution)/shard_map/while/body/eval_jaxpr/sub | solution.py:31
  672.1 19.9 %multiply_subtract_fusion.198 = (f32[256]{0:T(256)S(1)}, f32[256]{0:T(256)S(1)}, f32[256]{0:T(256)S(1)}, f32[256]{0:T(256)S(1)}, f32[256]{0:T(256)S(1)}, /*index...) fusion(f32[256]{0:T(256)S(1)} %bitcast.1284, ...), kind=kLoop, calls=%fused_computation.101.clone.1 | loop fusion | flops 16384 | bytes 66688 | tf_op jit(solution)/shard_map/while/body/eval_jaxpr/sub | solution.py:31
  693.7 19.9 %multiply_subtract_fusion.198 = (f32[256]{0:T(256)S(1)}, f32[256]{0:T(256)S(1)}, f32[256]{0:T(256)S(1)}, f32[256]{0:T(256)S(1)}, f32[256]{0:T(256)S(1)}, /*index...) fusion(f32[256]{0:T(256)S(1)} %bitcast.1284, ...), kind=kLoop, calls=%fused_computation.101.clone.1 | loop fusion | flops 16384 | bytes 66688 | tf_op jit(solution)/shard_map/while/body/eval_jaxpr/sub | solution.py:31
  715.4 19.9 %multiply_subtract_fusion.198 = (f32[256]{0:T(256)S(1)}, f32[256]{0:T(256)S(1)}, f32[256]{0:T(256)S(1)}, f32[256]{0:T(256)S(1)}, f32[256]{0:T(256)S(1)}, /*index...) fusion(f32[256]{0:T(256)S(1)} %bitcast.1284, ...), kind=kLoop, calls=%fused_computation.101.clone.1 | loop fusion | flops 16384 | bytes 66688 | tf_op jit(solution)/shard_map/while/body/eval_jaxpr/sub | solution.py:31
  735.4 1.5 multiply_subtract_fusion.72
  737.7 19.5 %multiply_subtract_fusion.41 = (f32[256]{0:T(256)S(1)}, f32[256]{0:T(256)S(1)}, f32[256]{0:T(256)S(1)}, f32[256]{0:T(256)S(1)}, f32[256]{0:T(256)S(1)}, /*index=...) fusion(f32[256]{0:T(256)S(1)} %bitcast.1377, ...), kind=kLoop, calls=%fused_computation.194 | loop fusion | flops 15872 | bytes 64636 | tf_op jit(solution)/shard_map/eval_jaxpr/sub | solution.py:31
  758.2 273.9 %all-reduce.2.cloned.1.call-done = f32[24,3,16,128]{3,2,1,0:T(8,128)} async-done(((f32[24,3,16,128]{3,2,1,0:T(8,128)}), f32[24,3,16,128]{3,2,1,0:T(8,128)}) %all-reduce.2.cloned.1.call-update) | async-done | bytes 589840 | tf_op jit(solution)/shard_map/psum | solution.py:16
  1032.0 1.1 reduce_sum.45
  1035.8 1.1 copy.14
  1036.9 9.6 all-to-all-start
  1047.3 0.9 copy-done.2
  1048.4 1.0 fusion
  1049.3 21.2 %all-to-all-done = f32[128,2,3,256]{3,1,2,0:T(2,128)S(1)} async-done(((f32[128,2,3,256]{3,1,2,0:T(2,128)}), f32[128,2,3,256]{3,1,2,0:T(2,128)S(1)}, u32[]{:S(2)}, u32[]{:S(2)}) %all-to-all-start) | async-done | bytes 786464 | tf_op jit(solution)/shard_map/all_to_all | solution.py:98
  1070.8 1.4 reshape.378
  (204 shorter events, 47.3 us)
Async XLA Ops:
  7.2 1026.3 %copy-start = (f32[1,128,256]{2,1,0:T(8,128)S(1)}, f32[1,128,256]{2,1,0:T(8,128)}, u32[]{:S(2)}) copy-start(f32[1,128,256]{2,1,0:T(8,128)} %param.17) | copy-start | bytes 393220
  7.2 1024.9 %all-reduce.2.cloned.1.call-start = ((), (), s32[]{:S(2)}) async-start(), calls=%async_computation.1 | async-start | bytes 1179648 | tf_op jit(solution)/shard_map/psum | solution.py:16
  7.9 0.7 copy-start.4
  757.3 0.7 copy-start.6
  758.1 275.1 %copy-start.3 = (f32[1,16,32]{2,1,0:T(8,128)S(1)}, f32[1,16,32]{2,1,0:T(8,128)}, u32[]{:S(2)}) copy-start(f32[1,16,32]{2,1,0:T(8,128)} %param.16) | copy-start | bytes 6148
  1032.0 1.4 copy-start.1
  1033.7 0.7 copy-start.5
  1036.9 33.6 %all-to-all-start = ((f32[128,2,3,256]{3,1,2,0:T(2,128)}), f32[128,2,3,256]{3,1,2,0:T(2,128)S(1)}, u32[]{:S(2)}, u32[]{:S(2)}) async-start(f32[128,2,3,256]{3,1,2,0:T(2,128)} %copy.14), calls=%async_computation | async-start | bytes 1572864 | tf_op jit(solution)/shard_map/all_to_all | solution.py:98
  1047.3 0.9 copy-start.2
Sparse Core Ops, SparseCore 0:
  11.5 1020.5 all-reduce.1
where the time goes:
time: 1090 us; the launch traced here: 1080 us
  other arithmetic  340 us (31%)
  waiting for transfers between devices  295 us (27%)
  loops' own time  288 us (26%)
  between operations  92.9 us (9%)
  local copies, waits for them, and re-layouts  50.4 us (5%)
    another operation x2, loops' own time, compact_operator(): return lax.linalg.tridiagonal_solve(below_diag, middle, above_diag, bmatrix)  288 us
    psum x1, waiting for transfers between devices, spread(): return lax.psum(kept, axis)  274 us
    div x9, other arithmetic, compact_operator(): return lax.linalg.tridiagonal_solve(below_diag, middle, above_diag, bmatrix)  176 us
    sub x9, other arithmetic, compact_operator(): return lax.linalg.tridiagonal_solve(below_diag, middle, above_diag, bmatrix)  160 us
    slice x89, local copies, waits for them, and re-layouts, compact_operator(): return lax.linalg.tridiagonal_solve(below_diag, middle, above_diag, bmatrix)  40.1 us
  transfers between devices with their start and end apart: 2, of which 2 were waited for; matrix products, arithmetic and copies ran while one was open for 35% of the time, Pallas kernels for 0%

commit v1 on v0

--- a/solution.py
+++ b/solution.py
@@ -1,5 +1,6 @@
 import jax
 import jax.numpy as jnp
+import numpy as np
 from jax import lax
 from jax.sharding import PartitionSpec as P
 
@@ -17,18 +18,16 @@
 
 
 def compact_operator(count):
-    positions = jnp.arange(count)
+    positions = np.arange(count)
     offset = positions[None, :] - positions[:, None]
     bmatrix = (
-        jnp.where(offset == 1, FIRST_COEF, 0.0)
-        - jnp.where(offset == -1, FIRST_COEF, 0.0)
-        + jnp.where(offset == 2, SECOND_COEF, 0.0)
-        - jnp.where(offset == -2, SECOND_COEF, 0.0)
-    ).astype(jnp.float32)
-    below_diag = jnp.where(positions > 0, ALPHA_SIDE, 0.0).astype(jnp.float32)
-    above_diag = jnp.where(positions < count - 1, ALPHA_SIDE, 0.0).astype(jnp.float32)
-    middle = jnp.ones((count,), jnp.float32)
-    return lax.linalg.tridiagonal_solve(below_diag, middle, above_diag, bmatrix)
+        np.where(offset == 1, FIRST_COEF, 0.0)
+        - np.where(offset == -1, FIRST_COEF, 0.0)
+        + np.where(offset == 2, SECOND_COEF, 0.0)
+        - np.where(offset == -2, SECOND_COEF, 0.0)
+    )
+    amatrix = np.eye(count) + np.where(np.abs(offset) == 1, ALPHA_SIDE, 0.0)
+    return jnp.asarray(np.linalg.solve(amatrix, bmatrix).astype(np.float32))
 
 
 def derive_rows(matrix, field):
@@ -70,10 +69,8 @@
     face_rows,
     face_owner,
 ):
-    scaled = amplitudes[0][:, None, None, None] * modal_blocks[0]
-    root = owner_map[0]
-    received = spread(scaled, "grid", root)
-    shape_sum = jnp.sum(received, axis=0)
+    local_sum = jnp.sum(amplitudes[0][:, None, None, None] * modal_blocks[0], axis=0)
+    shape_sum = spread(local_sum, "grid", owner_map[0])
     spanwise = jnp.einsum("sr,cst->crt", span_interp[0], shape_sum, precision=lax.Precision.HIGHEST)
     displace = jnp.einsum("crt,tj->crj", spanwise, chord_interp[0], precision=lax.Precision.HIGHEST)
     coords = base_coords[0] + displace

time: 1090 us -> 596 us (0.55); the launches traced: 1080 us -> 596 us
  blocking collectives: 0 us -> 550 us
  other arithmetic: 340 us -> 1.45 us
  loops' own time: 288 us -> 0 us
  waiting for transfers between devices: 295 us -> 20.5 us
  between operations: 92.9 us -> 1.55 us
  local copies, waits for them, and re-layouts: 50.4 us -> 6.82 us
    psum x0 -> x1, blocking collectives: none -> 550 us  [spread(): return lax.psum(kept, axis)]
    another operation x2 -> x0, loops' own time: 288 us -> none  [compact_operator(): return lax.linalg.tridiagonal_solve(below_diag, middle, above_diag, bmatrix)]
    psum x1 -> x0, waiting for transfers between devices: 274 us -> none  [spread(): return lax.psum(kept, axis)]
    div x9 -> x0, other arithmetic: 176 us -> none  [compact_operator(): return lax.linalg.tridiagonal_solve(below_diag, middle, above_diag, bmatrix)]
    sub x11 -> x0, other arithmetic: 160 us -> none  [the longest x9 160 us: compact_operator(): return lax.linalg.tridiagonal_solve(below_diag, middle, above_diag, bmatrix)]
    slice x89 -> x0, local copies, waits for them, and re-layouts: 40.1 us -> none  [compact_operator(): return lax.linalg.tridiagonal_solve(below_diag, middle, above_diag, bmatrix)]
  transfers between devices with their start and end apart: 2 -> 1, of which waited for: 2 -> 1; matrix products, arithmetic and copies ran while one was open for 35% -> 0% of each run, Pallas kernels for 0% -> 0%
where the time goes in v1:
time: 596 us
  blocking collectives  550 us (92%)
  waiting for transfers between devices  20.5 us (3%)
  starting transfers between devices  12.2 us (2%)
  local copies, waits for them, and re-layouts  6.82 us (1%)
    psum x1, blocking collectives, spread(): return lax.psum(kept, axis)  550 us
    all_to_all x1, waiting for transfers between devices, body(): lax.all_to_all(outgoing, 'grid', split_axis=0, concat_axis=0, tiled=True)  20.5 us
    all_to_all x1, starting transfers between devices, body(): lax.all_to_all(outgoing, 'grid', split_axis=0, concat_axis=0, tiled=True)  12.2 us
  transfers between devices with their start and end apart: 1, of which 1 were waited for; matrix products, arithmetic and copies ran while one was open for 0% of the time, Pallas kernels for 0%

profile of v1, /device:TPU:1, one launch (start us, length us, event | category | flops | bytes accessed | tf_op | source)
XLA Modules:
  0.0 596.0 jit_solution(6915176428018133514)
XLA Ops:
  0.6 0.0 copy-start
  1.3 0.0 copy-start.9
  1.3 0.6 copy-done.9
  2.0 0.2 convert_reduce_fusion
  2.2 0.0 copy-start.8
  2.2 0.6 copy-done.8
  2.8 1.2 fusion.1
  4.0 0.0 copy-start.3
  4.1 550.4 %psum.7 = f32[3,16,128]{2,1,0:T(8,128)S(1)} all-reduce(f32[3,16,128]{2,1,0:T(8,128)S(1)} %broadcast_select_fusion), channel_id=1, replica_groups=mesh['blade'=4,'grid'=128] {'grid'}, use_global_device_ids=true, to_apply=%region_1.2 | all-reduce | flops 6144 | bytes 49152 | tf_op jit(solution)/shard_map/psum | solution.py:17
  554.4 0.0 copy-done.6
  554.4 0.2 convolution_bitcast_fusion.1
  554.7 0.0 copy-done
  554.7 0.2 convolution_add_fusion
  554.9 0.0 copy-start.7
  555.0 0.6 copy-done.7
  555.6 0.3 fusion.19
  555.9 0.6 fusion.7
  556.5 0.5 reshape.22
  557.0 1.1 copy.16
  558.2 12.2 %all-to-all-start = ((f32[128,2,3,256]{3,1,2,0:T(2,128)}), f32[128,2,3,256]{3,1,2,0:T(2,128)S(1)}, u32[]{:S(2)}, u32[]{:S(2)}) async-start(f32[128,2,3,256]{3,1,2,0:T(2,128)} %copy.16), calls=%async_computation | async-start | bytes 1572864 | tf_op jit(solution)/shard_map/all_to_all | solution.py:95
  570.3 0.2 convolution_bitcast_fusion
  570.6 0.0 copy-done.1
  570.6 0.4 fusion.25
  571.0 0.0 copy-start.4
  571.1 0.0 copy-start.2
  571.1 0.8 copy-done.4
  572.0 0.7 copy-done.10
  572.7 0.2 fusion.11
  572.8 1.0 fusion
  573.8 20.5 %all-to-all-done = f32[128,2,3,256]{3,1,2,0:T(2,128)S(1)} async-done(((f32[128,2,3,256]{3,1,2,0:T(2,128)}), f32[128,2,3,256]{3,1,2,0:T(2,128)S(1)}, u32[]{:S(2)}, u32[]{:S(2)}) %all-to-all-start) | async-done | bytes 786464 | tf_op jit(solution)/shard_map/all_to_all | solution.py:95
  594.3 0.3 copy.17
  594.5 1.4 reshape.23
  (14 shorter events, 0.1 us)
Async XLA Ops:
  0.6 554.1 %copy-start = (f32[1,128,256]{2,1,0:T(8,128)S(1)}, f32[1,128,256]{2,1,0:T(8,128)}, u32[]{:S(2)}) copy-start(f32[1,128,256]{2,1,0:T(8,128)} %param.15) | copy-start | bytes 393220
  1.3 0.7 copy-start.9
  2.2 0.7 copy-start.8
  2.8 551.6 %copy-start.6 = (f32[1,16,32]{2,1,0:T(8,128)S(1)}, f32[1,16,32]{2,1,0:T(8,128)}, u32[]{:S(2)}) copy-start(f32[1,16,32]{2,1,0:T(8,128)} %param.14) | copy-start | bytes 6148
  4.0 550.7 %copy-start.3 = (f32[1,3,32,256]{3,2,1,0:T(8,128)S(1)}, f32[1,3,32,256]{3,2,1,0:T(8,128)}, u32[]{:S(2)}) copy-start(f32[1,3,32,256]{3,2,1,0:T(8,128)} %param.16) | copy-start | bytes 294916
  554.9 0.7 copy-start.7
  558.2 12.2 %copy-start.5 = (f32[32,32,1]{1,0,2:T(8,128)S(1)}, f32[32,32,1]{1,0,2:T(8,128)}, u32[]{:S(2)}) copy-start(f32[32,32,1]{1,0,2:T(8,128)} %constant.29) | copy-start | bytes 12292
  558.2 12.4 %copy-start.1 = (f32[256,256,1]{1,0,2:T(8,128)S(1)}, f32[256,256,1]{1,0,2:T(8,128)}, u32[]{:S(2)}) copy-start(f32[256,256,1]{1,0,2:T(8,128)} %constant.28) | copy-start | bytes 786436
  558.2 36.1 %all-to-all-start = ((f32[128,2,3,256]{3,1,2,0:T(2,128)}), f32[128,2,3,256]{3,1,2,0:T(2,128)S(1)}, u32[]{:S(2)}, u32[]{:S(2)}) async-start(f32[128,2,3,256]{3,1,2,0:T(2,128)} %copy.16), calls=%async_computation | async-start | bytes 1572864 | tf_op jit(solution)/shard_map/all_to_all | solution.py:95
  571.0 0.9 copy-start.4
  571.1 1.7 copy-start.2
  571.9 0.7 copy-start.10

commit v2 on v1

v2 whole, which is shorter than its diff:
```python
import functools

import jax
import jax.numpy as jnp
import numpy as np
from jax import lax
from jax.experimental import pallas as pl
from jax.experimental.pallas import tpu as pltpu
from jax.sharding import PartitionSpec as P

ALPHA_SIDE = 1.0 / 3.0
FIRST_COEF = 7.0 / 9.0
SECOND_COEF = 1.0 / 36.0

MODES, SI, SJ = 24, 16, 128
LI, LJ = 32, 256
CAP, NF = 2, 96
NY, NZ, NX, NC = 8, 2, 4, 2
NP = NZ * NX * NC
MESH = pl.DeviceIdType.MESH
HIGHEST = lax.Precision.HIGHEST


def compact_operator(count):
    positions = np.arange(count)
    offset = positions[None, :] - positions[:, None]
    bmatrix = (
        np.where(offset == 1, FIRST_COEF, 0.0)
        - np.where(offset == -1, FIRST_COEF, 0.0)
        + np.where(offset == 2, SECOND_COEF, 0.0)
        - np.where(offset == -2, SECOND_COEF, 0.0)
    )
    amatrix = np.eye(count) + np.where(np.abs(offset) == 1, ALPHA_SIDE, 0.0)
    return np.linalg.solve(amatrix, bmatrix).astype(np.float32)


def dot(first, second):
    return jnp.dot(first, second, precision=HIGHEST, preferred_element_type=jnp.float32)


def cross_three(first, second):
    return [
        first[1] * second[2] - first[2] * second[1],
        first[2] * second[0] - first[0] * second[2],
        first[0] * second[1] - first[1] * second[0],
    ]


def dot_three(first, second):
    return first[0] * second[0] + first[1] * second[1] + first[2] * second[2]


def slot_table(rows, owner):
    faces = lax.broadcasted_iota(jnp.int32, (1, NF), 1)
    code = (faces * 64 + rows).astype(jnp.float32)
    both = jnp.concatenate([code, owner.astype(jnp.float32)], axis=0)
    both = jnp.concatenate([both, jnp.zeros((6, NF), jnp.float32)], axis=0)
    both = jnp.concatenate([both, jnp.zeros((8, 128 - NF), jnp.float32)], axis=1)
    cols = jnp.transpose(both)[:NF]
    code_col, owner_col = cols[:, 0:1], cols[:, 1:2]
    slots = lax.broadcasted_iota(jnp.int32, (NF, NY * NP * CAP), 1)
    hit = owner_col == (slots // CAP).astype(jnp.float32)
    big = 1.0e6
    first = jnp.min(jnp.where(hit, code_col, big), axis=0, keepdims=True)
    last = jnp.max(jnp.where(hit, code_col, -1.0), axis=0, keepdims=True)
    lane = lax.broadcasted_iota(jnp.int32, (1, NY * NP * CAP), 1)
    is_first = lane % CAP == 0
    pick = jnp.where(is_first, first, last)
    pick_row = pick - 64.0 * jnp.floor(pick * (1.0 / 64.0))
    margin = jnp.where(is_first, last + 1.0, last - first)
    return jnp.where(margin > 0.0, pick_row, float(LI))


def kernel(
    amp_ref,
    root_ref,
    modal_hbm,
    span_hbm,
    chord_hbm,
    base_hbm,
    flow_hbm,
    rows_ref,
    owner_ref,
    op_rows_ref,
    op_cols_hbm,
    result_ref,
    fringe_hbm,
    modal,
    span,
    chord,
    base,
    flow,
    op_cols,
    chunk_out,
    chunk_in,
    pick_out,
    pick_in,
    part_out,
    part_in,
    table_out,
    table_in,
    block,
    chosen,
    load_sem,
    phase_send,
    phase_recv,
    table_send,
    table_recv,
    ring_send,
    ring_recv,
    plane_send,
    plane_recv,
    self_sem,
):
    me = lax.axis_index("grid")
    my_y, my_p = me // NP, me % NP
    my_z, my_x, my_c = my_p // (NX * NC), (my_p // NC) % NX, my_p % NC

    def at_y(step):
        return lax.rem(my_y + step, NY)

    def device_y(step):
        return {"grid": at_y(step) * NP + my_p}

    offsets = [(dz, dx, dc) for dz in range(NZ) for dx in range(NX) for dc in range(NC)][1:]
    peers = [
        (lax.rem(my_z + dz, NZ) * NX + lax.rem(my_x + dx, NX)) * NC + lax.rem(my_c + dc, NC)
        for dz, dx, dc in offsets
    ]

    def device_p(peer):
        return {"grid": my_y * NP + peer}

    barrier = pltpu.get_barrier_semaphore()
    for peer in peers:
        pl.semaphore_signal(barrier, inc=1, device_id=device_p(peer), device_id_type=MESH)
    for step in range(1, NY):
        pl.semaphore_signal(barrier, inc=1, device_id=device_y(step), device_id_type=MESH)

    loads = [
        pltpu.make_async_copy(source, target, load_sem.at[number])
        for number, (source, target) in enumerate(
            [
                (modal_hbm, modal),
                (span_hbm, span),
                (chord_hbm, chord),
                (base_hbm, base),
                (flow_hbm, flow),
                (op_cols_hbm, op_cols),
            ]
        )
    ]
    for load in loads:
        load.start()

    table = slot_table(rows_ref[...], owner_ref[...])
    table_out[...] = table
    table_in[0] = table

    loads[0].wait()
    shape = amp_ref[0, 0] * modal[0]
    for mode in range(1, MODES):
        shape = shape + amp_ref[0, mode] * modal[mode]
    for s in range(SI):
        for comp in range(3):
            chunk_out[s, comp : comp + 1, :] = shape[comp, s : s + 1, :]
    chunk_in[my_p] = chunk_out[my_p]

    pl.semaphore_wait(barrier, len(peers) + NY - 1)

    root_y, root_p = root_ref[0] // NP, root_ref[0] % NP

    def exchange_plane(source_of, target, number):
        copies = [
            pltpu.make_async_remote_copy(
                src_ref=source_of(peer),
                dst_ref=target.at[my_p],
                send_sem=phase_send.at[number],
                recv_sem=phase_recv.at[number],
                device_id=device_p(peer),
                device_id_type=MESH,
            )
            for peer in peers
        ]
        for copy in copies:
            copy.start()

    def await_all(ref, send_sem, recv_sem):
        pltpu.make_async_copy(ref, ref, recv_sem).wait()
        pltpu.make_async_copy(ref, ref, send_sem).wait()

    exchange_plane(lambda peer: chunk_out.at[peer], chunk_in, 0)

    for step in range(1, NY):
        pltpu.make_async_remote_copy(
            src_ref=table_out,
            dst_ref=table_in.at[step],
            send_sem=table_send,
            recv_sem=table_recv,
            device_id=device_y(step),
            device_id_type=MESH,
        ).start()

    await_all(chunk_in.at[pl.ds(0, NP - 1)], phase_send.at[0], phase_recv.at[0])
    picked = chunk_in[root_p]
    pick_out[...] = picked
    pick_in[my_y] = picked
    for step in range(1, NY):
        pltpu.make_async_remote_copy(
            src_ref=pick_out,
            dst_ref=pick_in.at[my_y],
            send_sem=phase_send.at[1],
            recv_sem=phase_recv.at[1],
            device_id=device_y(step),
            device_id_type=MESH,
        ).start()
    await_all(pick_in.at[pl.ds(0, NY - 1)], phase_send.at[1], phase_recv.at[1])
    part = pick_in[root_y]
    part_out[...] = part
    part_in[my_p] = part
    exchange_plane(lambda peer: part_out, part_in, 2)

    await_all(table_in.at[pl.ds(0, NY - 1)], table_send, table_recv)
    tables = pltpu.roll(table_in[:, 0, :], lax.rem(NY - my_y, NY) * (NP * CAP), 1)
    table_cols = jnp.transpose(tables[:, :128])[: NP * CAP]

    for load in loads[1:]:
        load.wait()
    await_all(part_in.at[pl.ds(0, NP - 1)], phase_send.at[2], phase_recv.at[2])

    for comp in range(3):
        spanwise = lax.dot_general(
            span[...],
            part_in[:, comp, :],
            (((0,), (0,)), ((), ())),
            precision=HIGHEST,
            preferred_element_type=jnp.float32,
        )
        block[0, comp] = base[comp] + dot(spanwise, chord[...])

    def ring(index, comp, forward, half=False):
        later = lax.rem(index + (1 if forward else NY - 1), NY)
        source, target = block.at[index, comp], block.at[later, comp]
        if half:
            rows = pl.ds(0 if forward else LI // 2, LI // 2)
            source, target = source.at[rows], target.at[rows]
        way = 0 if forward else 1
        hop = later if forward else NY - later
        return pltpu.make_async_remote_copy(
            src_ref=source,
            dst_ref=target,
            send_sem=ring_send.at[way, hop - 1, comp],
            recv_sem=ring_recv.at[way, hop - 1, comp],
            device_id=device_y(1 if forward else NY - 1),
            device_id_type=MESH,
        )

    sent = []

    def send_ring(index, comp, forward, half=False):
        copy = ring(index, comp, forward, half)
        copy.start()
        sent.append(copy)

    def choose(index):
        lanes = lax.broadcasted_iota(jnp.int32, (NP * CAP, 3 * LI), 1) % LI
        hot = table_cols[:, index : index + 1] == lanes.astype(jnp.float32)
        hot = jnp.where(hot, 1.0, 0.0).astype(jnp.bfloat16)
        for comp in range(3):
            values = block[index, comp]
            high = values.astype(jnp.bfloat16)
            rest = values - high.astype(jnp.float32)
            middle = rest.astype(jnp.bfloat16)
            low = (rest - middle.astype(jnp.float32)).astype(jnp.bfloat16)
            stacked = jnp.concatenate([high, middle, low], axis=0)
            slots = jnp.dot(hot, stacked, preferred_element_type=jnp.float32)
            for peer in range(NP):
                chosen[index, peer, comp] = slots[CAP * peer : CAP * peer + CAP]
        donor = at_y(NY - index)
        for peer in peers:
            pltpu.make_async_remote_copy(
                src_ref=chosen.at[index, peer],
                dst_ref=fringe_hbm.at[donor, my_p],
                send_sem=plane_send,
                recv_sem=plane_recv,
                device_id=device_p(peer),
                device_id_type=MESH,
            ).start()
        copy = pltpu.make_async_copy(
            chosen.at[index, my_p], fringe_hbm.at[donor, my_p], self_sem.at[index]
        )
        copy.start()
        return copy

    for comp in range(3):
        send_ring(0, comp, True)
        send_ring(0, comp, False)
    own = [choose(0)]

    coords = [block[0, comp] for comp in range(3)]
    along_rows = [dot(op_rows_ref[...], coords[comp]) for comp in range(3)]
    along_cols = [dot(coords[comp], op_cols[...]) for comp in range(3)]
    normal = cross_three(along_rows, along_cols)
    weight = 1.0 + dot_three(normal, normal)
    stream = [flow[comp] for comp in range(3)]
    flux_rows = dot_three(stream, cross_three(along_cols, normal)) / weight
    flux_cols = dot_three(stream, cross_three(normal, along_rows)) / weight
    result_ref[...] = dot(op_rows_ref[...], flux_rows) + dot(flux_cols, op_cols[...])

    for hop in range(1, NY // 2 + 1):
        last = hop == NY // 2
        for comp in range(3):
            ring(hop - 1, comp, True, last).wait_recv()
            if not last:
                send_ring(hop, comp, True, hop == NY // 2 - 1)
            ring((NY - hop + 1) % NY, comp, False, last).wait_recv()
            if not last:
                send_ring(NY - hop, comp, False, hop == NY // 2 - 1)
        own.append(choose(hop))
        if not last:
            own.append(choose(NY - hop))

    for copy in sent:
        copy.wait_send()
    for copy in own:
        copy.wait()
    await_all(chosen.at[:, pl.ds(0, NP - 1)], plane_send, plane_recv)


def body(
    modal_blocks,
    amplitudes,
    owner_map,
    span_interp,
    chord_interp,
    base_coords,
    flow_state,
    face_rows,
    face_owner,
):
    op_rows = jnp.asarray(compact_operator(LI))
    op_cols = jnp.asarray(np.ascontiguousarray(compact_operator(LJ).T))
    vmem = pl.BlockSpec(memory_space=pltpu.VMEM)
    smem = pl.BlockSpec(memory_space=pltpu.SMEM)
    hbm = pl.BlockSpec(memory_space=pl.ANY)
    f32 = jnp.float32
    result, fringe = pl.pallas_call(
        kernel,
        out_shape=(
            jax.ShapeDtypeStruct((LI, LJ), f32),
            jax.ShapeDtypeStruct((NY, NP, 3, CAP, LJ), f32),
        ),
        in_specs=[smem, smem, hbm, hbm, hbm, hbm, hbm, vmem, vmem, vmem, hbm],
        out_specs=(vmem, hbm),
        scratch_shapes=[
            pltpu.VMEM((MODES, 3, SI, SJ), f32),
            pltpu.VMEM((SI, LI), f32),
            pltpu.VMEM((SJ, LJ), f32),
            pltpu.VMEM((3, LI, LJ), f32),
            pltpu.VMEM((3, LI, LJ), f32),
            pltpu.VMEM((LJ, LJ), f32),
            pltpu.VMEM((NP, 3, SJ), f32),
            pltpu.VMEM((NP, 3, SJ), f32),
            pltpu.VMEM((3, SJ), f32),
            pltpu.VMEM((NY, 3, SJ), f32),
            pltpu.VMEM((3, SJ), f32),
            pltpu.VMEM((NP, 3, SJ), f32),
            pltpu.VMEM((1, NY * NP * CAP), f32),
            pltpu.VMEM((NY, 1, NY * NP * CAP), f32),
            pltpu.VMEM((NY, 3, LI, LJ), f32),
            pltpu.VMEM((NY, NP, 3, CAP, LJ), f32),
            pltpu.SemaphoreType.DMA((6,)),
            pltpu.SemaphoreType.DMA((3,)),
            pltpu.SemaphoreType.DMA((3,)),
            pltpu.SemaphoreType.DMA,
            pltpu.SemaphoreType.DMA,
            pltpu.SemaphoreType.DMA((2, 4, 3)),
            pltpu.SemaphoreType.DMA((2, 4, 3)),
            pltpu.SemaphoreType.DMA,
            pltpu.SemaphoreType.DMA,
            pltpu.SemaphoreType.DMA((NY,)),
        ],
        compiler_params=pltpu.CompilerParams(collective_id=0, has_side_effects=True),
        name="section",
    )(
        amplitudes,
        owner_map,
        modal_blocks[0],
        span_interp[0],
        chord_interp[0],
        base_coords[0],
        flow_state[0],
        face_rows,
        face_owner.reshape(1, NF),
        op_rows,
        op_cols,
    )
    fringe = fringe.reshape(NY * NP, 3, CAP, LJ).transpose(0, 2, 1, 3)
    return (result[None], fringe.reshape(1, NY * NP * CAP, 3, LJ))


def solution(mesh):
    return jax.shard_map(
        body,
        mesh=mesh,
        in_specs=(
            P("blade", "grid", None, None, None),
            P("blade", None),
            P("blade"),
            P("blade", None, "grid"),
            P("blade", "grid", None),
            P("blade", None, "grid", None),
            P("blade", None, "grid", None),
            P("blade", "grid"),
            P("blade", "grid", None),
        ),
        out_specs=(P("blade", "grid", None), P("blade", "grid", None, None)),
        check_vma=False,
    )
```

time: 596 us -> 49 us (0.08)
  blocking collectives: 550 us -> 0 us
  Pallas kernels: 0 us -> 44 us
  waiting for transfers between devices: 20.5 us -> 0 us
  starting transfers between devices: 12.2 us -> 0 us
    psum x1 -> x0, blocking collectives: 550 us -> none  [spread(): return lax.psum(kept, axis)]
    pallas_call x0 -> x1, Pallas kernels: none -> 44 us  [body(): pl.pallas_call(kernel, out_shape=(jax.ShapeDtypeStruct((LI, LJ), f32), ja...]
    all_to_all x1 -> x0, waiting for transfers between devices: 20.5 us -> none  [body(): lax.all_to_all(outgoing, 'grid', split_axis=0, concat_axis=0, tiled=True)]
    all_to_all x1 -> x0, starting transfers between devices: 12.2 us -> none  [body(): lax.all_to_all(outgoing, 'grid', split_axis=0, concat_axis=0, tiled=True)]
  transfers between devices with their start and end apart: 1 -> 0, of which waited for: 1 -> 0; matrix products, arithmetic and copies ran while one was open for 0% -> 0% of each run, Pallas kernels for 0% -> 0%
where the time goes in v2:
time: 49 us; the launch traced here: 48.7 us
  Pallas kernels  44 us (90%)
  local copies, waits for them, and re-layouts  3.44 us (7%)
  between operations  1.3 us (3%)
    pallas_call x1, Pallas kernels, body(): pl.pallas_call(kernel, out_shape=(jax.ShapeDtypeStruct((LI, LJ), f32), ja...  44 us
    reshape x1, local copies, waits for them, and re-layouts, body(): return (result[None], fringe.reshape(1, NY * NP * CAP, 3, LJ))  1.42 us
    transpose x1, local copies, waits for them, and re-layouts, body(): fringe = fringe.reshape(NY * NP, 3, CAP, LJ).transpose(0, 2, 1, 3)  1.4 us

profile of v2, /device:TPU:1, one launch (start us, length us, event | category | flops | bytes accessed | tf_op | source)
XLA Modules:
  0.0 48.7 jit_solution(8287885802737532645)
XLA Ops:
  1.3 44.0 %section.1 = (f32[32,256]{1,0:T(8,128)}, f32[8,16,3,2,256]{4,3,2,1,0:T(2,128)}) custom-call(f32[1,24]{1,0:T(1,128)} %amp_ref.1, s32[1]{0:T(128)S(6)} %copy.15.root_ref, f32[24,3,16,128]{3,2,1,0:T(8,128)} %bitcast.13, f32[16,32]{1,0:T(8,128)} %bitcast.18, f32[128,256]{1,0:T(8,128)} %bitcast.14, f32[3,32,256]{2,1,0:T(8,128)} %bitcast.15, ...), custom_call_target="tpu_custom_call" | custom-call | tf_op jit(solution)/shard_map/section/pallas_call | solution.py:347
  45.3 1.4 %copy.13 = f32[128,2,3,256]{3,1,0,2:T(2,128)S(1)} copy(f32[128,2,3,256]{3,1,2,0:T(2,128)} %bitcast.12) | data formatting | bytes 1572864 | tf_op jit(solution)/shard_map/transpose | solution.py:398
  46.7 0.0 copy-start
  46.7 1.4 %reshape.15 = f32[1,256,3,256]{3,1,2,0:T(8,128)} reshape(f32[128,2,3,256]{3,1,0,2:T(2,128)S(1)} %copy.13) | data formatting | bytes 1572864 | tf_op jit(solution)/shard_map/reshape | solution.py:399
  48.1 0.0 copy-done
  48.1 0.6 %copy.16 = f32[1,32,256]{2,1,0:T(8,128)} copy(f32[1,32,256]{2,1,0:T(8,128)S(1)} %bitcast.17) | data formatting | bytes 65536
Async XLA Ops:
  46.7 1.4 %copy-start = (f32[32,256]{1,0:T(8,128)S(1)}, f32[32,256]{1,0:T(8,128)}, u32[]{:S(2)}) copy-start(f32[32,256]{1,0:T(8,128)} %get-tuple-element.4) | copy-start | bytes 98308

commit v3 on v2

v3 whole, which is shorter than its diff:
```python
import jax
import jax.numpy as jnp
import numpy as np
from jax import lax
from jax.experimental import pallas as pl
from jax.experimental.pallas import tpu as pltpu
from jax.sharding import PartitionSpec as P

ALPHA_SIDE = 1.0 / 3.0
FIRST_COEF = 7.0 / 9.0
SECOND_COEF = 1.0 / 36.0

MODES, SI, SJ = 24, 16, 128
LI, LJ = 32, 256
CAP, NF = 2, 96
NY, NZ, NX, NC = 8, 2, 4, 2
NP = NZ * NX * NC
MESH = pl.DeviceIdType.MESH
HIGHEST = lax.Precision.HIGHEST


def compact_operator(count):
    positions = np.arange(count)
    offset = positions[None, :] - positions[:, None]
    bmatrix = (
        np.where(offset == 1, FIRST_COEF, 0.0)
        - np.where(offset == -1, FIRST_COEF, 0.0)
        + np.where(offset == 2, SECOND_COEF, 0.0)
        - np.where(offset == -2, SECOND_COEF, 0.0)
    )
    amatrix = np.eye(count) + np.where(np.abs(offset) == 1, ALPHA_SIDE, 0.0)
    return np.linalg.solve(amatrix, bmatrix).astype(np.float32)


def dot(first, second):
    return jnp.dot(first, second, precision=HIGHEST, preferred_element_type=jnp.float32)


def cross_three(first, second):
    return [
        first[1] * second[2] - first[2] * second[1],
        first[2] * second[0] - first[0] * second[2],
        first[0] * second[1] - first[1] * second[0],
    ]


def dot_three(first, second):
    return first[0] * second[0] + first[1] * second[1] + first[2] * second[2]


def slot_table(rows, owner):
    faces = lax.broadcasted_iota(jnp.int32, (1, NF), 1)
    code = (faces * 64 + rows).astype(jnp.float32)
    both = jnp.concatenate([code, owner.astype(jnp.float32)], axis=0)
    both = jnp.concatenate([both, jnp.zeros((6, NF), jnp.float32)], axis=0)
    both = jnp.concatenate([both, jnp.zeros((8, 128 - NF), jnp.float32)], axis=1)
    cols = jnp.transpose(both)[:NF]
    code_col, owner_col = cols[:, 0:1], cols[:, 1:2]
    slots = lax.broadcasted_iota(jnp.int32, (NF, NY * NP * CAP), 1)
    hit = owner_col == (slots // CAP).astype(jnp.float32)
    big = 1.0e6
    first = jnp.min(jnp.where(hit, code_col, big), axis=0, keepdims=True)
    last = jnp.max(jnp.where(hit, code_col, -1.0), axis=0, keepdims=True)
    lane = lax.broadcasted_iota(jnp.int32, (1, NY * NP * CAP), 1)
    is_first = lane % CAP == 0
    pick = jnp.where(is_first, first, last)
    pick_row = pick - 64.0 * jnp.floor(pick * (1.0 / 64.0))
    margin = jnp.where(is_first, last + 1.0, last - first)
    return jnp.where(margin > 0.0, pick_row, float(LI))


def kernel(
    root_hbm,
    amp_hbm,
    rows_hbm,
    owner_hbm,
    modal_hbm,
    span_hbm,
    chord_hbm,
    base_hbm,
    flow_hbm,
    op_rows_hbm,
    op_cols_hbm,
    result_hbm,
    fringe_hbm,
    root_ref,
    amp_ref,
    rows_ref,
    owner_ref,
    modal,
    span,
    chord,
    base,
    flow,
    op_rows_ref,
    op_cols,
    result,
    local_sum,
    core_in,
    chip_in,
    plane_in,
    shape_in,
    table_out,
    table_in,
    block,
    chosen,
    load_sem,
    phase_send,
    phase_recv,
    table_send,
    table_recv,
    ring_send,
    ring_recv,
    plane_send,
    plane_recv,
    self_sem,
    result_sem,
):
    me = lax.axis_index("grid")
    my_y, my_p = me // NP, me % NP
    my_q, my_c = my_p // NC, my_p % NC
    my_z, my_x = my_q // NX, my_q % NX

    def at_y(step):
        return lax.rem(my_y + step, NY)

    def device_y(step):
        return {"grid": at_y(step) * NP + my_p}

    def peer_at(dz, dx, dc):
        z, x, c = lax.rem(my_z + dz, NZ), lax.rem(my_x + dx, NX), lax.rem(my_c + dc, NC)
        return (z * NX + x) * NC + c

    def device_p(peer):
        return {"grid": my_y * NP + peer}

    far_first = [(dz, dx) for dz in (1, 0) for dx in (2, 1, 3, 0)]
    peers = [peer_at(dz, dx, dc) for dc in (1, 0) for dz, dx in far_first][:-1]
    chips = [peer_at(dz, dx, 0) for dz, dx in far_first][:-1]
    partner = peer_at(0, 0, 1)
    y_steps = (4, 3, 5, 2, 6, 1, 7)

    loads = [
        pltpu.make_async_copy(source, target, load_sem.at[number])
        for number, (source, target) in enumerate(
            [
                (modal_hbm, modal),
                (root_hbm, root_ref),
                (amp_hbm, amp_ref),
                (rows_hbm, rows_ref),
                (owner_hbm, owner_ref),
                (span_hbm, span),
                (chord_hbm, chord),
                (base_hbm, base),
                (flow_hbm, flow),
                (op_rows_hbm, op_rows_ref),
                (op_cols_hbm, op_cols),
            ]
        )
    ]
    for load in loads[:5]:
        load.start()

    barrier = pltpu.get_barrier_semaphore()
    for step in y_steps:
        pl.semaphore_signal(barrier, inc=1, device_id=device_y(step), device_id_type=MESH)
    for peer in peers:
        pl.semaphore_signal(barrier, inc=1, device_id=device_p(peer), device_id_type=MESH)

    for load in loads[1:5]:
        load.wait()
    table = slot_table(rows_ref[...], owner_ref[...])
    table_out[...] = table
    table_in[0] = table

    loads[0].wait()
    for load in loads[5:]:
        load.start()
    shape = amp_ref[0, 0] * modal[0]
    for mode in range(1, MODES):
        shape = shape + amp_ref[0, mode] * modal[mode]
    shape = shape.reshape(3 * SI, SJ)
    half_rows = 3 * SI // NC
    for half in range(NC):
        local_sum[half] = shape[half * half_rows : (half + 1) * half_rows]
    core_in[my_c] = local_sum[my_c]

    pl.semaphore_wait(barrier, len(peers) + len(y_steps))

    root = root_ref[0]
    root_y, root_q, root_c = root // NP, (root % NP) // NC, root % NC

    def send(source, target, number, device):
        pltpu.make_async_remote_copy(
            src_ref=source,
            dst_ref=target,
            send_sem=phase_send.at[number],
            recv_sem=phase_recv.at[number],
            device_id=device,
            device_id_type=MESH,
        ).start()

    def await_all(ref, send_sem, recv_sem):
        pltpu.make_async_copy(ref, ref, recv_sem).wait()
        pltpu.make_async_copy(ref, ref, send_sem).wait()

    send(local_sum.at[1 - my_c], core_in.at[my_c], 0, device_p(partner))
    await_all(core_in.at[0], phase_send.at[0], phase_recv.at[0])
    chip_in[my_q] = core_in[root_c]
    for peer in chips:
        send(chip_in.at[my_q], chip_in.at[my_q], 1, device_p(peer))
    for step in y_steps:
        pltpu.make_async_remote_copy(
            src_ref=table_out,
            dst_ref=table_in.at[step],
            send_sem=table_send,
            recv_sem=table_recv,
            device_id=device_y(step),
            device_id_type=MESH,
        ).start()
    await_all(chip_in.at[pl.ds(0, NP // NC - 1)], phase_send.at[1], phase_recv.at[1])
    plane_in[my_y] = chip_in[root_q]
    for step in y_steps:
        send(plane_in.at[my_y], plane_in.at[my_y], 2, device_y(step))

    await_all(table_in.at[pl.ds(0, NY - 1)], table_send, table_recv)
    tables = pltpu.roll(table_in[:, 0, :], lax.rem(NY - my_y, NY) * (NP * CAP), 1)
    table_cols = jnp.transpose(tables[:, :128])[: NP * CAP]
    for load in loads[5:]:
        load.wait()

    await_all(plane_in.at[pl.ds(0, NY - 1)], phase_send.at[2], phase_recv.at[2])
    shape_in[my_c] = plane_in[root_y]
    send(shape_in.at[my_c], shape_in.at[my_c], 3, device_p(partner))
    await_all(shape_in.at[0], phase_send.at[3], phase_recv.at[3])
    shape_sum = shape_in[...].reshape(3 * SI, SJ)

    def ring(index, comp, half, forward, step=1):
        later = (index + (step if forward else NY - step)) % NY
        rows = pl.ds(half * (LI // 2), LI // 2)
        way = 0 if forward else 1
        hop = later if forward else NY - later
        return pltpu.make_async_remote_copy(
            src_ref=block.at[index, comp, rows],
            dst_ref=block.at[later, comp, rows],
            send_sem=ring_send.at[way, hop - 1, comp * 2 + half],
            recv_sem=ring_recv.at[way, hop - 1, comp * 2 + half],
            device_id=device_y(step if forward else NY - step),
            device_id_type=MESH,
        )

    sent = []

    def send_ring(index, comp, half, forward, step=1):
        copy = ring(index, comp, half, forward, step)
        copy.start()
        sent.append(copy)

    def hot_rows(index):
        lanes = lax.broadcasted_iota(jnp.int32, (NP * CAP, 3 * LI), 1) % LI
        hot = table_cols[:, index : index + 1] == lanes.astype(jnp.float32)
        return jnp.where(hot, 1.0, 0.0).astype(jnp.bfloat16)

    own = []

    def slots_of(donor):
        return pl.ds(pl.multiple_of((donor * NP + my_p) * CAP, CAP), CAP)

    def choose(index, comp, hot):
        values = block[index, comp]
        high = values.astype(jnp.bfloat16)
        rest = values - high.astype(jnp.float32)
        middle = rest.astype(jnp.bfloat16)
        low = (rest - middle.astype(jnp.float32)).astype(jnp.bfloat16)
        stacked = jnp.concatenate([high, middle, low], axis=0)
        slots = jnp.dot(hot, stacked, preferred_element_type=jnp.float32)
        for peer in range(NP):
            chosen[index, comp, peer] = slots[CAP * peer : CAP * peer + CAP]
        place = slots_of(at_y(NY - index))
        single = index in (3, 4, 5)
        if comp < 2 and not single:
            return
        comps = comp if single else slice(None)
        for peer in peers:
            pltpu.make_async_remote_copy(
                src_ref=chosen.at[index, comps, peer],
                dst_ref=fringe_hbm.at[comps, place],
                send_sem=plane_send,
                recv_sem=plane_recv,
                device_id=device_p(peer),
                device_id_type=MESH,
            ).start()
        if comp == 2:
            copy = pltpu.make_async_copy(
                chosen.at[index, :, my_p], fringe_hbm.at[:, place], self_sem.at[index]
            )
            copy.start()
            own.append(copy)

    for comp in range(3):
        spanwise = lax.dot_general(
            span[...],
            shape_sum[comp * SI : (comp + 1) * SI],
            (((0,), (0,)), ((), ())),
            precision=HIGHEST,
            preferred_element_type=jnp.float32,
        )
        block[0, comp] = base[comp] + dot(spanwise, chord[...])
        for half in range(2):
            send_ring(0, comp, half, True)
            send_ring(0, comp, half, False)
    hot = hot_rows(0)
    for comp in range(3):
        choose(0, comp, hot)

    coords = [block[0, comp] for comp in range(3)]
    along_rows = [dot(op_rows_ref[...], coords[comp]) for comp in range(3)]
    along_cols = [dot(coords[comp], op_cols[...]) for comp in range(3)]
    normal = cross_three(along_rows, along_cols)
    weight = 1.0 + dot_three(normal, normal)
    stream = [flow[comp] for comp in range(3)]
    flux_rows = dot_three(stream, cross_three(along_cols, normal)) / weight
    flux_cols = dot_three(stream, cross_three(normal, along_rows)) / weight
    result[...] = dot(op_rows_ref[...], flux_rows) + dot(flux_cols, op_cols[...])
    leave = pltpu.make_async_copy(result, result_hbm, result_sem)
    leave.start()

    for hop in range(1, NY // 2 + 1):
        last = hop == NY // 2
        hot_up, hot_down = hot_rows(hop), hot_rows(NY - hop)
        for comp in range(3):
            for half in range(2):
                if last:
                    ring(2 if half == 0 else NY - 2, comp, half, half == 0, 2).wait_recv()
                    continue
                ring(hop - 1, comp, half, True).wait_recv()
                if hop < 3:
                    send_ring(hop, comp, half, True)
                if hop == 2 and half == 0:
                    send_ring(hop, comp, half, True, 2)
                ring((NY - hop + 1) % NY, comp, half, False).wait_recv()
                if hop < 3:
                    send_ring(NY - hop, comp, half, False)
                if hop == 2 and half == 1:
                    send_ring(NY - hop, comp, half, False, 2)
            choose(hop, comp, hot_up)
            if not last:
                choose(NY - hop, comp, hot_down)

    for copy in sent:
        copy.wait_send()
    for copy in own:
        copy.wait()
    leave.wait()
    await_all(chosen.at[:, :, pl.ds(0, NP - 1)], plane_send, plane_recv)


def body(
    modal_blocks,
    amplitudes,
    owner_map,
    span_interp,
    chord_interp,
    base_coords,
    flow_state,
    face_rows,
    face_owner,
):
    op_rows = jnp.asarray(compact_operator(LI))
    op_cols = jnp.asarray(np.ascontiguousarray(compact_operator(LJ).T))
    hbm = pl.BlockSpec(memory_space=pltpu.HBM)
    free = pl.BlockSpec(memory_space=pl.ANY)
    f32 = jnp.float32
    result, fringe = pl.pallas_call(
        kernel,
        out_shape=(
            jax.ShapeDtypeStruct((LI, LJ), f32),
            jax.ShapeDtypeStruct((3, NY * NP * CAP, LJ), f32),
        ),
        in_specs=[free] + [hbm] * 10,
        out_specs=(free, free),
        scratch_shapes=[
            pltpu.SMEM((1,), jnp.int32),
            pltpu.SMEM((1, MODES), f32),
            pltpu.VMEM((1, NF), jnp.int32),
            pltpu.VMEM((1, NF), jnp.int32),
            pltpu.VMEM((MODES, 3, SI, SJ), f32),
            pltpu.VMEM((SI, LI), f32),
            pltpu.VMEM((SJ, LJ), f32),
            pltpu.VMEM((3, LI, LJ), f32),
            pltpu.VMEM((3, LI, LJ), f32),
            pltpu.VMEM((LI, LI), f32),
            pltpu.VMEM((LJ, LJ), f32),
            pltpu.VMEM((LI, LJ), f32),
            pltpu.VMEM((NC, 3 * SI // NC, SJ), f32),
            pltpu.VMEM((NC, 3 * SI // NC, SJ), f32),
            pltpu.VMEM((NP // NC, 3 * SI // NC, SJ), f32),
            pltpu.VMEM((NY, 3 * SI // NC, SJ), f32),
            pltpu.VMEM((NC, 3 * SI // NC, SJ), f32),
            pltpu.VMEM((1, NY * NP * CAP), f32),
            pltpu.VMEM((NY, 1, NY * NP * CAP), f32),
            pltpu.VMEM((NY, 3, LI, LJ), f32),
            pltpu.VMEM((NY, 3, NP, CAP, LJ), f32),
            pltpu.SemaphoreType.DMA((11,)),
            pltpu.SemaphoreType.DMA((4,)),
            pltpu.SemaphoreType.DMA((4,)),
            pltpu.SemaphoreType.DMA,
            pltpu.SemaphoreType.DMA,
            pltpu.SemaphoreType.DMA((2, 4, 6)),
            pltpu.SemaphoreType.DMA((2, 4, 6)),
            pltpu.SemaphoreType.DMA,
            pltpu.SemaphoreType.DMA,
            pltpu.SemaphoreType.DMA((NY,)),
            pltpu.SemaphoreType.DMA,
        ],
        compiler_params=pltpu.CompilerParams(collective_id=0, has_side_effects=True, vmem_limit_bytes=12 << 20),
        name="section",
    )(
        owner_map,
        *(
            pltpu.with_memory_space_constraint(array, pltpu.HBM)
            for array in (
                amplitudes,
                face_rows,
                face_owner.reshape(1, NF),
                modal_blocks[0],
                span_interp[0],
                chord_interp[0],
                base_coords[0],
                flow_state[0],
                op_rows,
                op_cols,
            )
        ),
    )
    return (result[None], fringe.transpose(1, 0, 2)[None])


def solution(mesh):
    return jax.shard_map(
        body,
        mesh=mesh,
        in_specs=(
            P("blade", "grid", None, None, None),
            P("blade", None),
            P("blade"),
            P("blade", None, "grid"),
            P("blade", "grid", None),
            P("blade", None, "grid", None),
            P("blade", None, "grid", None),
            P("blade", "grid"),
            P("blade", "grid", None),
        ),
        out_specs=(P("blade", "grid", None), P("blade", "grid", None, None)),
        check_vma=False,
    )
```

time: 49 us -> 42.6 us (0.87)
  Pallas kernels: 44 us -> 39.7 us
  local copies, waits for them, and re-layouts: 3.44 us -> 1.5 us
    pallas_call x1, Pallas kernels: 44 us -> 39.7 us  [body(): pl.pallas_call(kernel, out_shape=(jax.ShapeDtypeStruct((LI, LJ), f32), ja...]
    reshape x1 -> x0, local copies, waits for them, and re-layouts: 1.42 us -> none  [body(): return (result[None], fringe.reshape(1, NY * NP * CAP, 3, LJ))]
    transpose x1 -> x0, local copies, waits for them, and re-layouts: 1.4 us -> none  [body(): fringe = fringe.reshape(NY * NP, 3, CAP, LJ).transpose(0, 2, 1, 3)]
    unnamed x3 -> x2, local copies, waits for them, and re-layouts: 0.62 us -> 1.5 us
where the time goes in v3:
time: 42.6 us; the launch traced here: 42.4 us
  Pallas kernels  39.7 us (93%)
  local copies, waits for them, and re-layouts  1.5 us (4%)
  between operations  1.29 us (3%)
    pallas_call x1, Pallas kernels, body(): pl.pallas_call(kernel, out_shape=(jax.ShapeDtypeStruct((LI, LJ), f32), ja...  39.7 us
    unnamed x2, local copies, waits for them, and re-layouts  1.5 us

profile of v3, /device:TPU:1, one launch (start us, length us, event | category | flops | bytes accessed | tf_op | source)
XLA Modules:
  0.0 42.4 jit_solution(5221761056686454934)
XLA Ops:
  1.3 39.7 %section.1 = (f32[32,256]{1,0:T(8,128)S(1)}, f32[3,256,256]{2,1,0:T(8,128)S(1)}) custom-call(s32[1]{0:T(128)S(6)} %copy.15.root_hbm, f32[1,24]{1,0:T(1,128)} %amp_hbm.1, s32[1,96]{1,0:T(1,128)} %rows_hbm.1, s32[1,96]{1,0:T(1,128)} %bitcast.17, f32[24,3,16,128]{3,2,1,0:T(8,128)} %bitcast.12, f32[16,32]{1,0:T(8,128)} %bitcast.16, f32[128,256]{1,0:T(8,128)} %bitcast.13, ...), custom_call_target="tpu_custom_call" | custom-call | tf_op jit(solution)/shard_map/section/pallas_call | solution.py:374
  40.9 0.6 %copy.16 = f32[1,32,256]{2,1,0:T(8,128)} copy(f32[1,32,256]{2,1,0:T(8,128)S(1)} %bitcast.11) | data formatting | bytes 65536
  41.6 0.9 %copy.17 = f32[1,256,3,256]{3,1,2,0:T(8,128)} copy(f32[1,256,3,256]{3,1,2,0:T(8,128)S(1)} %bitcast.10) | data formatting | bytes 1572864

commit v4 on v3

--- a/solution.py
+++ b/solution.py
@@ -94,6 +94,9 @@
     flow,
     op_rows_ref,
     op_cols,
+    near_span,
+    near_chord,
+    near_base,
     result,
     local_sum,
     core_in,
@@ -115,6 +118,8 @@
     plane_recv,
     self_sem,
     result_sem,
+    near_send,
+    near_recv,
 ):
     me = lax.axis_index("grid")
     my_y, my_p = me // NP, me % NP
@@ -205,6 +210,22 @@
         pltpu.make_async_copy(ref, ref, send_sem).wait()
 
     send(local_sum.at[1 - my_c], core_in.at[my_c], 0, device_p(partner))
+    near = [
+        pltpu.make_async_remote_copy(
+            src_ref=source,
+            dst_ref=target.at[way],
+            send_sem=near_send.at[way, number],
+            recv_sem=near_recv.at[way, number],
+            device_id=device_y(1 if way == 0 else NY - 1),
+            device_id_type=MESH,
+        )
+        for number, (source, target) in enumerate(
+            [(span_hbm, near_span), (chord_hbm, near_chord), (base_hbm, near_base)]
+        )
+        for way in range(2)
+    ]
+    for copy in near:
+        copy.start()
     await_all(core_in.at[0], phase_send.at[0], phase_recv.at[0])
     chip_in[my_q] = core_in[root_c]
     for peer in chips:
@@ -232,6 +253,8 @@
     await_all(plane_in.at[pl.ds(0, NY - 1)], phase_send.at[2], phase_recv.at[2])
     shape_in[my_c] = plane_in[root_y]
     send(shape_in.at[my_c], shape_in.at[my_c], 3, device_p(partner))
+    for copy in near:
+        copy.wait()
     await_all(shape_in.at[0], phase_send.at[3], phase_recv.at[3])
     shape_sum = shape_in[...].reshape(3 * SI, SJ)
 
@@ -297,21 +320,31 @@
             copy.start()
             own.append(copy)
 
-    for comp in range(3):
-        spanwise = lax.dot_general(
-            span[...],
-            shape_sum[comp * SI : (comp + 1) * SI],
-            (((0,), (0,)), ((), ())),
-            precision=HIGHEST,
-            preferred_element_type=jnp.float32,
-        )
-        block[0, comp] = base[comp] + dot(spanwise, chord[...])
-        for half in range(2):
-            send_ring(0, comp, half, True)
-            send_ring(0, comp, half, False)
-    hot = hot_rows(0)
-    for comp in range(3):
-        choose(0, comp, hot)
+    def displaced(index, span_of, chord_of, base_of):
+        spanwise = [
+            lax.dot_general(
+                span_of[...],
+                shape_sum[comp * SI : (comp + 1) * SI],
+                (((0,), (0,)), ((), ())),
+                precision=HIGHEST,
+                preferred_element_type=jnp.float32,
+            )
+            for comp in range(3)
+        ]
+        moved = dot(jnp.concatenate(spanwise, axis=0), chord_of[...])
+        for comp in range(3):
+            block[index, comp] = base_of[comp] + moved[comp * LI : (comp + 1) * LI]
+
+    for way, index in ((0, 1), (1, NY - 1)):
+        displaced(index, near_span.at[way], near_chord.at[way], near_base.at[way])
+        for comp in range(3):
+            for half in range(2):
+                send_ring(index, comp, half, way == 0)
+    displaced(0, span, chord, base)
+    for index in (1, NY - 1, 0):
+        hot = hot_rows(index)
+        for comp in range(3):
+            choose(index, comp, hot)
 
     coords = [block[0, comp] for comp in range(3)]
     along_rows = [dot(op_rows_ref[...], coords[comp]) for comp in range(3)]
@@ -325,7 +358,7 @@
     leave = pltpu.make_async_copy(result, result_hbm, result_sem)
     leave.start()
 
-    for hop in range(1, NY // 2 + 1):
+    for hop in range(2, NY // 2 + 1):
         last = hop == NY // 2
         hot_up, hot_down = hot_rows(hop), hot_rows(NY - hop)
         for comp in range(3):
@@ -391,6 +424,9 @@
             pltpu.VMEM((3, LI, LJ), f32),
             pltpu.VMEM((LI, LI), f32),
             pltpu.VMEM((LJ, LJ), f32),
+            pltpu.VMEM((2, SI, LI), f32),
+            pltpu.VMEM((2, SJ, LJ), f32),
+            pltpu.VMEM((2, 3, LI, LJ), f32),
             pltpu.VMEM((LI, LJ), f32),
             pltpu.VMEM((NC, 3 * SI // NC, SJ), f32),
             pltpu.VMEM((NC, 3 * SI // NC, SJ), f32),
@@ -412,6 +448,8 @@
             pltpu.SemaphoreType.DMA,
             pltpu.SemaphoreType.DMA((NY,)),
             pltpu.SemaphoreType.DMA,
+            pltpu.SemaphoreType.DMA((2, 3)),
+            pltpu.SemaphoreType.DMA((2, 3)),
         ],
         compiler_params=pltpu.CompilerParams(collective_id=0, has_side_effects=True, vmem_limit_bytes=12 << 20),
         name="section",

time: 42.6 us -> 40.2 us (0.944)
  Pallas kernels: 39.7 us -> 37.2 us
    pallas_call x1, Pallas kernels: 39.7 us -> 37.2 us  [body(): pl.pallas_call(kernel, out_shape=(jax.ShapeDtypeStruct((LI, LJ), f32), ja...]
where the time goes in v4:
time: 40.2 us; the launch traced here: 40 us
  Pallas kernels  37.2 us (93%)
  local copies, waits for them, and re-layouts  1.5 us (4%)
  between operations  1.29 us (3%)
    pallas_call x1, Pallas kernels, body(): pl.pallas_call(kernel, out_shape=(jax.ShapeDtypeStruct((LI, LJ), f32), ja...  37.2 us
    unnamed x2, local copies, waits for them, and re-layouts  1.5 us

profile of v4, /device:TPU:1, one launch (start us, length us, event | category | flops | bytes accessed | tf_op | source)
XLA Modules:
  0.0 40.0 jit_solution(7141307596221626478)
XLA Ops:
  1.3 37.2 %section.1 = (f32[32,256]{1,0:T(8,128)S(1)}, f32[3,256,256]{2,1,0:T(8,128)S(1)}) custom-call(s32[1]{0:T(128)S(6)} %copy.15.root_hbm, f32[1,24]{1,0:T(1,128)} %amp_hbm.1, s32[1,96]{1,0:T(1,128)} %rows_hbm.1, s32[1,96]{1,0:T(1,128)} %bitcast.17, f32[24,3,16,128]{3,2,1,0:T(8,128)} %bitcast.12, f32[16,32]{1,0:T(8,128)} %bitcast.16, f32[128,256]{1,0:T(8,128)} %bitcast.13, ...), custom_call_target="tpu_custom_call" | custom-call | tf_op jit(solution)/shard_map/section/pallas_call | solution.py:407
  38.5 0.6 %copy.16 = f32[1,32,256]{2,1,0:T(8,128)} copy(f32[1,32,256]{2,1,0:T(8,128)S(1)} %bitcast.11) | data formatting | bytes 65536
  39.1 0.9 %copy.17 = f32[1,256,3,256]{3,1,2,0:T(8,128)} copy(f32[1,256,3,256]{3,1,2,0:T(8,128)S(1)} %bitcast.10) | data formatting | bytes 1572864

commit v5 on v4

--- a/solution.py
+++ b/solution.py
@@ -34,6 +34,11 @@
 
 def dot(first, second):
     return jnp.dot(first, second, precision=HIGHEST, preferred_element_type=jnp.float32)
+
+
+def split(values):
+    high = values.astype(jnp.bfloat16)
+    return high, (values - high.astype(jnp.float32)).astype(jnp.bfloat16)
 
 
 def cross_three(first, second):
@@ -97,6 +102,8 @@
     near_span,
     near_chord,
     near_base,
+    span_parts,
+    chord_parts,
     result,
     local_sum,
     core_in,
@@ -220,10 +227,12 @@
             device_id_type=MESH,
         )
         for number, (source, target) in enumerate(
-            [(span_hbm, near_span), (chord_hbm, near_chord), (base_hbm, near_base)]
+            [(span, near_span), (chord, near_chord), (base, near_base)]
         )
         for way in range(2)
     ]
+    for load in loads[5:8]:
+        load.wait()
     for copy in near:
         copy.start()
     await_all(core_in.at[0], phase_send.at[0], phase_recv.at[0])
@@ -247,7 +256,7 @@
     await_all(table_in.at[pl.ds(0, NY - 1)], table_send, table_recv)
     tables = pltpu.roll(table_in[:, 0, :], lax.rem(NY - my_y, NY) * (NP * CAP), 1)
     table_cols = jnp.transpose(tables[:, :128])[: NP * CAP]
-    for load in loads[5:]:
+    for load in loads[8:]:
         load.wait()
 
     await_all(plane_in.at[pl.ds(0, NY - 1)], phase_send.at[2], phase_recv.at[2])
@@ -255,6 +264,13 @@
     send(shape_in.at[my_c], shape_in.at[my_c], 3, device_p(partner))
     for copy in near:
         copy.wait()
+    for number, (span_of, chord_of) in enumerate(
+        [(near_span.at[0], near_chord.at[0]), (near_span.at[1], near_chord.at[1]), (span, chord)]
+    ):
+        high, low = split(span_of[...])
+        span_parts[number] = jnp.concatenate([high, high, low], axis=0)
+        high, low = split(chord_of[...])
+        chord_parts[number] = jnp.concatenate([high, low, high], axis=0)
     await_all(shape_in.at[0], phase_send.at[3], phase_recv.at[3])
     shape_sum = shape_in[...].reshape(3 * SI, SJ)
 
@@ -320,27 +336,36 @@
             copy.start()
             own.append(copy)
 
-    def displaced(index, span_of, chord_of, base_of):
-        spanwise = [
-            lax.dot_general(
-                span_of[...],
-                shape_sum[comp * SI : (comp + 1) * SI],
-                (((0,), (0,)), ((), ())),
-                precision=HIGHEST,
-                preferred_element_type=jnp.float32,
-            )
-            for comp in range(3)
-        ]
-        moved = dot(jnp.concatenate(spanwise, axis=0), chord_of[...])
+    parts = [split(shape_sum[comp * SI : (comp + 1) * SI]) for comp in range(3)]
+    wide_high = jnp.concatenate([high for high, _ in parts], axis=1)
+    wide_low = jnp.concatenate([low for _, low in parts], axis=1)
+    wide = jnp.concatenate([wide_high, wide_low, wide_high], axis=0)
+
+    def displaced(index, number, base_of):
+        spanwise = lax.dot_general(
+            span_parts[number],
+            wide,
+            (((0,), (0,)), ((), ())),
+            preferred_element_type=jnp.float32,
+        )
+        stacked = jnp.concatenate(
+            [spanwise[:, comp * SJ : (comp + 1) * SJ] for comp in range(3)], axis=0
+        )
+        high, low = split(stacked)
+        moved = jnp.dot(
+            jnp.concatenate([high, high, low], axis=1),
+            chord_parts[number],
+            preferred_element_type=jnp.float32,
+        )
         for comp in range(3):
             block[index, comp] = base_of[comp] + moved[comp * LI : (comp + 1) * LI]
 
     for way, index in ((0, 1), (1, NY - 1)):
-        displaced(index, near_span.at[way], near_chord.at[way], near_base.at[way])
+        displaced(index, way, near_base.at[way])
         for comp in range(3):
             for half in range(2):
                 send_ring(index, comp, half, way == 0)
-    displaced(0, span, chord, base)
+    displaced(0, 2, base)
     for index in (1, NY - 1, 0):
         hot = hot_rows(index)
         for comp in range(3):
@@ -386,6 +411,17 @@
         copy.wait()
     leave.wait()
     await_all(chosen.at[:, :, pl.ds(0, NP - 1)], plane_send, plane_recv)
+
+
+def leave(result_in, fringe_in, result_out, fringe_out, sem):
+    copies = [
+        pltpu.make_async_copy(result_in, result_out, sem.at[0]),
+        pltpu.make_async_copy(fringe_in, fringe_out, sem.at[1]),
+    ]
+    for copy in copies:
+        copy.start()
+    for copy in copies:
+        copy.wait()
 
 
 def body(
@@ -427,6 +463,8 @@
             pltpu.VMEM((2, SI, LI), f32),
             pltpu.VMEM((2, SJ, LJ), f32),
             pltpu.VMEM((2, 3, LI, LJ), f32),
+            pltpu.VMEM((3, 3 * SI, LI), jnp.bfloat16),
+            pltpu.VMEM((3, 3 * SJ, LJ), jnp.bfloat16),
             pltpu.VMEM((LI, LJ), f32),
             pltpu.VMEM((NC, 3 * SI // NC, SJ), f32),
             pltpu.VMEM((NC, 3 * SI // NC, SJ), f32),
@@ -471,6 +509,18 @@
             )
         ),
     )
+    result, fringe = pl.pallas_call(
+        leave,
+        out_shape=(
+            jax.ShapeDtypeStruct(result.shape, f32),
+            jax.ShapeDtypeStruct(fringe.shape, f32),
+        ),
+        in_specs=[free, free],
+        out_specs=(hbm, hbm),
+        scratch_shapes=[pltpu.SemaphoreType.DMA((2,))],
+        compiler_params=pltpu.CompilerParams(vmem_limit_bytes=1 << 20),
+        name="leave",
+    )(result, fringe)
     return (result[None], fringe.transpose(1, 0, 2)[None])
 
 

time: 40.2 us -> 39.1 us (0.973)
  local copies, waits for them, and re-layouts: 1.5 us -> 0 us
  Pallas kernels: 37.2 us -> 37.7 us
    unnamed x2 -> x0, local copies, waits for them, and re-layouts: 1.5 us -> none
    pallas_call x0 -> x1, Pallas kernels: none -> 0.91 us  [body(): pl.pallas_call(leave, out_shape=(jax.ShapeDtypeStruct(result.shape, f32),...]
    pallas_call x1, Pallas kernels: 37.2 us -> 36.8 us  [body(): pl.pallas_call(kernel, out_shape=(jax.ShapeDtypeStruct((LI, LJ), f32), ja...]
where the time goes in v5:
time: 39.1 us; the launch traced here: 39 us
  Pallas kernels  37.7 us (96%)
  between operations  1.29 us (3%)
    pallas_call x1, Pallas kernels, body(): pl.pallas_call(kernel, out_shape=(jax.ShapeDtypeStruct((LI, LJ), f32), ja...  36.8 us
    pallas_call x1, Pallas kernels, body(): pl.pallas_call(leave, out_shape=(jax.ShapeDtypeStruct(result.shape, f32),...  0.91 us

profile of v5, /device:TPU:1, one launch (start us, length us, event | category | flops | bytes accessed | tf_op | source)
XLA Modules:
  0.0 39.0 jit_solution(8178901572590562662)
XLA Ops:
  1.3 36.8 %section.1 = (f32[32,256]{1,0:T(8,128)S(1)}, f32[3,256,256]{2,1,0:T(8,128)S(1)}) custom-call(s32[1]{0:T(128)S(6)} %copy.13.root_hbm, f32[1,24]{1,0:T(1,128)} %amp_hbm.1, s32[1,96]{1,0:T(1,128)} %rows_hbm.1, s32[1,96]{1,0:T(1,128)} %bitcast.15, f32[24,3,16,128]{3,2,1,0:T(8,128)} %bitcast.10, f32[16,32]{1,0:T(8,128)} %bitcast.14, f32[128,256]{1,0:T(8,128)} %bitcast.11, ...), custom_call_target="tpu_custom_call" | custom-call | tf_op jit(solution)/shard_map/section/pallas_call | solution.py:443
  38.1 0.9 %leave.1 = (f32[32,256]{1,0:T(8,128)}, f32[3,256,256]{2,1,0:T(8,128)}) custom-call(f32[32,256]{1,0:T(8,128)S(1)} %get-tuple-element.6.result_in, f32[3,256,256]{2,1,0:T(8,128)S(1)} %get-tuple-element.7.fringe_in), custom_call_target="tpu_custom_call" | custom-call | tf_op jit(solution)/shard_map/leave/pallas_call | solution.py:512

commit v6 on v5

--- a/solution.py
+++ b/solution.py
@@ -233,7 +233,7 @@
     ]
     for load in loads[5:8]:
         load.wait()
-    for copy in near:
+    for copy in near[:4]:
         copy.start()
     await_all(core_in.at[0], phase_send.at[0], phase_recv.at[0])
     chip_in[my_q] = core_in[root_c]
@@ -252,6 +252,8 @@
     plane_in[my_y] = chip_in[root_q]
     for step in y_steps:
         send(plane_in.at[my_y], plane_in.at[my_y], 2, device_y(step))
+    for copy in near[4:]:
+        copy.start()
 
     await_all(table_in.at[pl.ds(0, NY - 1)], table_send, table_recv)
     tables = pltpu.roll(table_in[:, 0, :], lax.rem(NY - my_y, NY) * (NP * CAP), 1)
@@ -259,18 +261,20 @@
     for load in loads[8:]:
         load.wait()
 
-    await_all(plane_in.at[pl.ds(0, NY - 1)], phase_send.at[2], phase_recv.at[2])
-    shape_in[my_c] = plane_in[root_y]
-    send(shape_in.at[my_c], shape_in.at[my_c], 3, device_p(partner))
-    for copy in near:
-        copy.wait()
-    for number, (span_of, chord_of) in enumerate(
-        [(near_span.at[0], near_chord.at[0]), (near_span.at[1], near_chord.at[1]), (span, chord)]
-    ):
+    def split_parts(number, span_of, chord_of):
         high, low = split(span_of[...])
         span_parts[number] = jnp.concatenate([high, high, low], axis=0)
         high, low = split(chord_of[...])
         chord_parts[number] = jnp.concatenate([high, low, high], axis=0)
+
+    split_parts(2, span, chord)
+    await_all(plane_in.at[pl.ds(0, NY - 1)], phase_send.at[2], phase_recv.at[2])
+    shape_in[my_c] = plane_in[root_y]
+    send(shape_in.at[my_c], shape_in.at[my_c], 3, device_p(partner))
+    for copy in near[:4]:
+        copy.wait()
+    for way in range(2):
+        split_parts(way, near_span.at[way], near_chord.at[way])
     await_all(shape_in.at[0], phase_send.at[3], phase_recv.at[3])
     shape_sum = shape_in[...].reshape(3 * SI, SJ)
 
@@ -361,6 +365,7 @@
             block[index, comp] = base_of[comp] + moved[comp * LI : (comp + 1) * LI]
 
     for way, index in ((0, 1), (1, NY - 1)):
+        near[4 + way].wait()
         displaced(index, way, near_base.at[way])
         for comp in range(3):
             for half in range(2):

time: 39.1 us -> 39.1 us (level)
  no operation moved by 1% of the time
where the time goes in v6:
time: 39.1 us; the launch traced here: 39 us
  Pallas kernels  37.7 us (96%)
  between operations  1.29 us (3%)
    pallas_call x1, Pallas kernels, body(): pl.pallas_call(kernel, out_shape=(jax.ShapeDtypeStruct((LI, LJ), f32), ja...  36.8 us
    pallas_call x1, Pallas kernels, body(): pl.pallas_call(leave, out_shape=(jax.ShapeDtypeStruct(result.shape, f32),...  0.91 us

profile of v6, /device:TPU:1, one launch (start us, length us, event | category | flops | bytes accessed | tf_op | source)
XLA Modules:
  0.0 39.0 jit_solution(15169659707939935508)
XLA Ops:
  1.3 36.8 %section.1 = (f32[32,256]{1,0:T(8,128)S(1)}, f32[3,256,256]{2,1,0:T(8,128)S(1)}) custom-call(s32[1]{0:T(128)S(6)} %copy.13.root_hbm, f32[1,24]{1,0:T(1,128)} %amp_hbm.1, s32[1,96]{1,0:T(1,128)} %rows_hbm.1, s32[1,96]{1,0:T(1,128)} %bitcast.15, f32[24,3,16,128]{3,2,1,0:T(8,128)} %bitcast.10, f32[16,32]{1,0:T(8,128)} %bitcast.14, f32[128,256]{1,0:T(8,128)} %bitcast.11, ...), custom_call_target="tpu_custom_call" | custom-call | tf_op jit(solution)/shard_map/section/pallas_call | solution.py:448
  38.1 0.9 %leave.1 = (f32[32,256]{1,0:T(8,128)}, f32[3,256,256]{2,1,0:T(8,128)}) custom-call(f32[32,256]{1,0:T(8,128)S(1)} %get-tuple-element.6.result_in, f32[3,256,256]{2,1,0:T(8,128)S(1)} %get-tuple-element.7.fringe_in), custom_call_target="tpu_custom_call" | custom-call | tf_op jit(solution)/shard_map/leave/pallas_call | solution.py:517
